TPU v7x, 128 devices: a whole 4x4x4 slice. The times are simulated.
128 devices in a mesh: row: 8 (over y, core), col: 16 (over z, x).
Axes of the slice: x: 4, y: 4, z: 4, core: 2. Of those that a mesh axis runs over, the one named last changes fastest.
Arguments:
- ancestor_inverse: float32 [12288, 12288], P('row', 'col')
- factor: bfloat16 [3, 12288, 512], P(None, ('row', 'col')), may hold values from -0.5 to 0.5
- coupling: float32 [3, 512, 512], replicated, may hold values from -0.25 to 0.25
- diagonal_inverse: float32 [3, 512, 512], replicated, may hold values from -6 to 6
- ancestors: int32 [3, 24], replicated, may hold values from -1 to 23, as said below
Outputs:
- block_columns: float32 [3, 12288, 512], P(None, ('row', 'col'))
- block_rows: float32 [3, 12288, 512], P(None, ('col', 'row'))
- node_blocks: float32 [3, 3, 512, 512], replicated
Inputs may be any that keep to these rules, and one draw needn't show every extreme that they name: `ancestors`: row k lists the ancestor block rows of supernode k, blocks of 512 rows: distinct indices in increasing order, then -1 in the slots left. Every block is listed by some supernode.
All inputs are finite; a program needn't handle non-finite values.
Results may differ from a plain program's by a relative error of at most 0.0003.
Values may be sent and summed in bfloat16 or wider, within the bound.
A program may use at most 128 MiB of HBM per device.

v0:
```python
import jax
import jax.numpy as jnp
from jax import lax
from jax.sharding import PartitionSpec as P

highest = lax.Precision.HIGHEST


def broadcast(value, axis, source):
    kept = jnp.where(lax.axis_index(axis) == source, value, 0).astype(value.dtype)
    return lax.psum(kept, axis)


def matmul(left, right):
    return jnp.dot(left, right, precision=highest)


def left_dot(left, right):
    return lax.dot_general(left, right, (((0,), (0,)), ((), ())), precision=highest)


def pair_index(later, earlier):
    return later * (later - 1) // 2 + earlier


def local(ancestor_inverse, factor, coupling, diagonal_inverse, ancestors):
    col_count = lax.axis_size("col")
    row_count = lax.axis_size("row")
    row_index = lax.axis_index("row")
    col_index = lax.axis_index("col")
    nodes_total, piece_rows, sn_width = factor.shape
    rows_here, cols_here = ancestor_inverse.shape
    group_ratio = rows_here // cols_here
    first_row = (row_index * col_count + col_index) * piece_rows
    block_of_row = (first_row + jnp.arange(piece_rows, dtype=jnp.int32)) // sn_width
    source_row = col_index // group_ratio
    block_start = col_index % group_ratio * cols_here
    row_layout = []
    solved = {}
    for current in range(nodes_total):
        listed = jnp.any(ancestors[current][:, None] == block_of_row[None, :], axis=0)
        lower_part = jnp.where(listed[:, None], factor[current], jnp.zeros_like(factor[current]))
        lower_rows = lax.all_gather(lower_part, "col", axis=0, tiled=True)
        own_block = lax.dynamic_slice_in_dim(lower_rows, block_start, cols_here, 0)
        lower_cols = broadcast(own_block, "row", source_row).astype(jnp.float32)
        lower_here = lower_part.astype(jnp.float32)
        product_sum = lax.psum_scatter(
            matmul(ancestor_inverse, lower_cols), "col", scatter_dimension=0, tiled=True
        )
        for earlier in range(current):
            product_sum = product_sum + matmul(
                row_layout[earlier], coupling[pair_index(current, earlier)]
            )
        column = -product_sum
        stacked = jnp.concatenate(row_layout + [column], axis=1)
        summed = lax.psum(left_dot(lower_here, stacked), ("row", "col"))
        crosses = [
            summed[:, earlier * sn_width : (earlier + 1) * sn_width] for earlier in range(current)
        ]
        self_term = summed[:, current * sn_width : (current + 1) * sn_width]
        for earlier in range(current):
            block_value = -crosses[earlier].T
            for inner in range(current):
                block_value = block_value - matmul(
                    solved[earlier, inner], coupling[pair_index(current, inner)]
                )
            solved[earlier, current] = block_value
            solved[current, earlier] = block_value.T
        diag_value = diagonal_inverse[current] - self_term
        for earlier in range(current):
            diag_value = diag_value - left_dot(
                coupling[pair_index(current, earlier)], solved[earlier, current]
            )
        solved[current, current] = diag_value
        row_layout.append(column)
    finished = jnp.stack(row_layout)
    part_rows = piece_rows // row_count
    ratio_cols = col_count // row_count
    split_parts = finished.reshape(nodes_total, row_count, part_rows, sn_width)
    held = lax.all_to_all(split_parts, "row", split_axis=1, concat_axis=1, tiled=True)
    targets = jnp.arange(row_count, dtype=jnp.int32) * ratio_cols + col_index // row_count
    onehot = (targets[:, None] == jnp.arange(col_count, dtype=jnp.int32)[None, :]).astype(
        jnp.float32
    )
    slotted = jnp.einsum("rc,nrqs->ncqs", onehot, held, precision=highest)
    arrived = lax.all_to_all(slotted, "col", split_axis=1, concat_axis=1, tiled=True)
    picked = lax.dynamic_slice_in_dim(arrived, col_index % ratio_cols * row_count, row_count, 1)
    landed = lax.all_to_all(picked, "row", split_axis=1, concat_axis=1, tiled=True)
    mirrored_all = landed.reshape(nodes_total, piece_rows, sn_width)
    node_blocks = jnp.stack(
        [
            jnp.stack([solved[first_node, second_node] for second_node in range(nodes_total)])
            for first_node in range(nodes_total)
        ]
    )
    return (finished, mirrored_all, node_blocks)


def solution(mesh):
    placed = (P("row", "col"), P(None, ("row", "col"), None), P(), P(), P())
    return jax.shard_map(
        local,
        mesh=mesh,
        in_specs=placed,
        out_specs=(P(None, ("row", "col"), None), P(None, ("col", "row"), None), P()),
        check_vma=False,
    )
```

profile of v0, /device:TPU:1, one launch (start us, length us, event | category | flops | bytes accessed | tf_op | source)
XLA Modules:
  0.0 691.0 jit_solution(10552824575240240170)
XLA Ops:
  11.5 45.6 %all-gather.6.cloned.1.call-done = bf16[1536,512]{1,0:T(8,128)(2,1)} async-done(((bf16[96,512]{1,0:T(8,128)(2,1)}), bf16[1536,512]{1,0:T(8,128)(2,1)}) %all-gather.6.cloned.1.call-update) | async-done | bytes 1572880 | tf_op jit(solution)/shard_map/all_gather | solution.py:43
  57.1 2.2 dynamic-slice_select_fusion.1
  59.2 43.3 %all-gather.4.cloned.1.call-done = bf16[1536,512]{1,0:T(8,128)(2,1)} async-done(((bf16[96,512]{1,0:T(8,128)(2,1)}), bf16[1536,512]{1,0:T(8,128)(2,1)}) %all-gather.4.cloned.1.call-update) | async-done | bytes 1572880 | tf_op jit(solution)/shard_map/all_gather | solution.py:43
  102.5 2.1 dynamic-slice_select_fusion.2
  104.7 43.3 %all-gather.8.cloned.1.call-done = bf16[1536,512]{1,0:T(8,128)(2,1)} async-done(((bf16[96,512]{1,0:T(8,128)(2,1)}), bf16[1536,512]{1,0:T(8,128)(2,1)}) %all-gather.8.cloned.1.call-update) | async-done | bytes 1572880 | tf_op jit(solution)/shard_map/all_gather | solution.py:43
  148.0 2.1 dynamic-slice_select_fusion
  150.3 66.0 %all-reduce.7.cloned.1.call-done = (bf16[768,512]{1,0:T(8,128)(2,1)}, bf16[768,512]{1,0:T(8,128)(2,1)}, bf16[768,512]{1,0:T(8,128)(2,1)}) async-done(((bf16[768,512]{1,0:T(8,128)(2,1)}, bf16[768,512]{1,0:T(8,128)(2,1)}, bf16[768,512]{1,0:T(8,128)(2,1)}), (bf16[768,512]{1,0:T(8,128)(2,1)}, bf16[768,512]{1,0:T(8,128)(2,1)}, bf16[768,512]{1,0:T(8,128)(2,1)})) %all-reduce.7.cloned.1.call-update) | async-done | bytes 2359312 | tf_op jit(solution)/shard_map/psum | solution.py:11
  216.2 6.7 convolution_bitcast_fusion.2
  222.9 2.3 copy.104
  225.3 6.7 convolution_bitcast_fusion.1
  232.0 2.4 copy.106
  234.5 6.7 convolution_bitcast_fusion
  241.2 2.4 copy.108
  244.1 57.1 %reduce-scatter.10.cloned.1.call-done = f32[96,512]{1,0:T(8,128)} async-done(((f32[1536,512]{1,0:T(8,128)}), f32[96,512]{1,0:T(8,128)}) %reduce-scatter.10.cloned.1.call-update) | async-done | bytes 196624 | tf_op jit(solution)/shard_map/reduce_scatter | solution.py:47
  301.2 78.3 %reduce-scatter.12.cloned.1.call-done = f32[96,512]{1,0:T(8,128)} async-done(((f32[1536,512]{1,0:T(8,128)}), f32[96,512]{1,0:T(8,128)}) %reduce-scatter.12.cloned.1.call-update) | async-done | bytes 196624 | tf_op jit(solution)/shard_map/reduce_scatter | solution.py:47
  381.3 77.3 %reduce-scatter.14.cloned.1.call-done = f32[96,512]{1,0:T(8,128)} async-done(((f32[1536,512]{1,0:T(8,128)}), f32[96,512]{1,0:T(8,128)}) %reduce-scatter.14.cloned.1.call-update) | async-done | bytes 196624 | tf_op jit(solution)/shard_map/reduce_scatter | solution.py:47
  458.6 1.8 convolution_add_fusion.1
  461.9 2.3 fusion.45
  464.2 3.1 fusion.38
  475.2 6.7 all-to-all-start
  481.9 15.6 %all-to-all-done = f32[3,8,12,512]{3,2,0,1:T(8,128)} async-done(((f32[3,8,12,512]{3,2,0,1:T(8,128)}), f32[3,8,12,512]{3,2,0,1:T(8,128)}, u32[]{:S(2)}, u32[]{:S(2)}) %all-to-all-start) | async-done | bytes 589856 | tf_op jit(solution)/shard_map/all_to_all | solution.py:80
  497.5 2.1 convolution_bitcast_fusion.3
  499.6 1.9 copy.80
  501.5 4.8 all-to-all-start.1
  506.3 21.0 %all-to-all-done.1 = f32[3,16,12,512]{3,2,0,1:T(8,128)} async-done(((f32[3,16,12,512]{3,2,0,1:T(8,128)}), f32[3,16,12,512]{3,2,0,1:T(8,128)}, u32[]{:S(2)}, u32[]{:S(2)}) %all-to-all-start.1) | async-done | bytes 1179680 | tf_op jit(solution)/shard_map/all_to_all | solution.py:86
  527.3 2.1 constant_dynamic-slice_fusion
  529.4 9.0 %all-to-all-start.2 = ((f32[3,8,12,512]{3,2,0,1:T(8,128)}), f32[3,8,12,512]{3,2,0,1:T(8,128)}, u32[]{:S(2)}, u32[]{:S(2)}) async-start(f32[3,8,12,512]{3,2,0,1:T(8,128)} %constant_dynamic-slice_fusion), calls=%async_computation.2 | async-start | bytes 1572864 | tf_op jit(solution)/shard_map/all_to_all | solution.py:88
  538.4 2.4 slice.71
  540.8 2.6 copy.110
  543.4 1.8 pad_maximum_fusion.2
  545.1 5.7 all-to-all-done.2
  550.9 2.2 copy.81
  553.0 2.0 reshape.46
  555.1 83.9 %all-reduce.5.cloned.1.call-done = (f32[512,1536]{1,0:T(8,128)}, f32[512,512]{1,0:T(8,128)}, f32[512,1024]{0,1:T(8,128)}) async-done(((f32[512,1536]{1,0:T(8,128)}, f32[512,512]{1,0:T(8,128)}, f32[512,1024]{0,1:T(8,128)}), (f32[512,1536]{1,0:T(8,128)}, f32[512,512]{1,0:T(8,128)}, f32[512,1024]{0,1:T(8,128)})) %all-reduce.5.cloned.1.call-update) | async-done | bytes 6291472 | tf_op jit(solution)/shard_map/psum | solution.py:56
  638.9 3.8 bitcast_subtract_fusion.7
  642.7 1.9 fusion.14
  644.6 1.9 fusion.18
  646.6 1.9 fusion.20
  648.5 2.0 fusion.3
  651.5 2.1 fusion.12
  653.7 3.1 fusion.2
  656.8 2.3 fusion.7
  659.1 2.3 fusion.60
  661.4 2.6 copy.85
  663.9 3.8 maximum_bitcast_fusion.1
  667.8 3.6 copy.95
  671.3 4.3 fusion.1
  679.1 4.9 pad_maximum_fusion
  (78 shorter events, 20.5 us)
Async XLA Ops:
  7.2 49.9 %all-gather.6.cloned.1.call-start = ((), (), s32[]{:S(2)}) async-start(), calls=%async_computation.7 | async-start | bytes 1671168 | tf_op jit(solution)/shard_map/all_gather | solution.py:43
  9.9 92.6 %all-gather.4.cloned.1.call-start = ((), (), s32[]{:S(2)}) async-start(), calls=%async_computation.6 | async-start | bytes 1671168 | tf_op jit(solution)/shard_map/all_gather | solution.py:43
  10.7 137.4 %all-gather.8.cloned.1.call-start = ((), (), s32[]{:S(2)}) async-start(), calls=%async_computation.8 | async-start | bytes 1671168 | tf_op jit(solution)/shard_map/all_gather | solution.py:43
  11.4 204.8 %all-reduce.7.cloned.1.call-start = ((), (), s32[]{:S(2)}) async-start(), calls=%async_computation.13 | async-start | bytes 4718592 | tf_op jit(solution)/shard_map/psum | solution.py:11
  150.2 151.0 %reduce-scatter.10.cloned.1.call-start = ((), (), s32[]{:S(2)}) async-start(), calls=%async_computation.9 | async-start | bytes 3342336 | tf_op jit(solution)/shard_map/reduce_scatter | solution.py:47
  225.3 154.3 %reduce-scatter.12.cloned.1.call-start = ((), (), s32[]{:S(2)}) async-start(), calls=%async_computation.10 | async-start | bytes 3342336 | tf_op jit(solution)/shard_map/reduce_scatter | solution.py:47
  234.4 224.1 %reduce-scatter.14.cloned.1.call-start = ((), (), s32[]{:S(2)}) async-start(), calls=%async_computation.11 | async-start | bytes 3342336 | tf_op jit(solution)/shard_map/reduce_scatter | solution.py:47
  243.6 136.0 %copy-start = (f32[3,512,512]{2,1,0:T(8,128)S(1)}, f32[3,512,512]{2,1,0:T(8,128)}, u32[]{:S(2)}) copy-start(f32[3,512,512]{2,1,0:T(8,128)} %param.7) | copy-start | bytes 9437188
  243.6 395.3 %all-reduce.5.cloned.1.call-start = ((), (), s32[]{:S(2)}) async-start(), calls=%async_computation.12 | async-start | bytes 12582912 | tf_op jit(solution)/shard_map/psum | solution.py:56
  301.2 159.9 %copy-start.16 = (f32[96,512]{1,0:T(8,128)S(1)}, f32[96,512]{1,0:T(8,128)}, u32[]{:S(2)}) copy-start(f32[96,512]{1,0:T(8,128)} %reduce-scatter.10.cloned.1.call-done) | copy-start | bytes 589828
  458.6 3.3 copy-start.20
  458.6 5.7 copy-start.22
  461.1 6.2 copy-start.17
  461.9 5.5 copy-start.19
  461.9 5.5 copy-start.21
  469.0 0.9 copy-start.18
  475.2 22.3 %all-to-all-start = ((f32[3,8,12,512]{3,2,0,1:T(8,128)}), f32[3,8,12,512]{3,2,0,1:T(8,128)}, u32[]{:S(2)}, u32[]{:S(2)}) async-start(f32[3,8,12,512]{3,2,0,1:T(8,128)} %copy.78), calls=%async_computation | async-start | bytes 1572864 | tf_op jit(solution)/shard_map/all_to_all | solution.py:80
  501.5 25.8 %all-to-all-start.1 = ((f32[3,16,12,512]{3,2,0,1:T(8,128)}), f32[3,16,12,512]{3,2,0,1:T(8,128)}, u32[]{:S(2)}, u32[]{:S(2)}) async-start(f32[3,16,12,512]{3,2,0,1:T(8,128)} %copy.80), calls=%async_computation.1 | async-start | bytes 3145728 | tf_op jit(solution)/shard_map/all_to_all | solution.py:86
  529.4 21.4 %all-to-all-start.2 = ((f32[3,8,12,512]{3,2,0,1:T(8,128)}), f32[3,8,12,512]{3,2,0,1:T(8,128)}, u32[]{:S(2)}, u32[]{:S(2)}) async-start(f32[3,8,12,512]{3,2,0,1:T(8,128)} %constant_dynamic-slice_fusion), calls=%async_computation.2 | async-start | bytes 1572864 | tf_op jit(solution)/shard_map/all_to_all | solution.py:88
  642.7 5.8 copy-start.1
  642.7 3.8 copy-start.8
  642.7 3.8 copy-start.9
  644.6 3.9 copy-start.10
  644.6 3.9 copy-start.11
  646.6 12.5 %copy-start.3 = (f32[512,512]{0,1:T(8,128)}, f32[512,512]{0,1:T(8,128)S(1)}, u32[]{:S(2)}) copy-start(f32[512,512]{0,1:T(8,128)S(1)} %fusion.18) | copy-start | bytes 3145732
  648.5 5.1 copy-start.6
  650.5 1.0 copy-start.7
  653.7 5.4 copy-start.4
  671.3 4.3 copy-start.2
  671.3 4.3 copy-start.12
  671.3 4.3 copy-start.15
  675.7 1.2 copy-start.13
  675.7 1.5 copy-start.14
  677.2 1.9 copy-start.5
Sparse Core Ops, SparseCore 0:
  10.7 46.3 all-gather.5
  59.2 43.3 all-gather.3
  104.7 43.3 all-gather.7
  151.0 65.1 all-reduce.6
  225.4 75.7 reduce-scatter.9
  304.4 75.1 reduce-scatter.11
  383.4 75.0 reduce-scatter.13
  469.1 169.7 all-reduce.4
where the time goes:
time: 699 us; the launch traced here: 691 us
  waiting for transfers between devices  539 us (77%)
  matrix products  54.5 us (8%)
  local copies, waits for them, and re-layouts  36 us (5%)
  other arithmetic  26 us (4%)
  starting transfers between devices  21.2 us (3%)
  between operations  14.7 us (2%)
    reduce_scatter x3, waiting for transfers between devices, local(): lax.psum_scatter(matmul(ancestor_inverse, lower_cols), 'col', scatter_dim...  213 us
    all_gather x3, waiting for transfers between devices, local(): lower_rows = lax.all_gather(lower_part, 'col', axis=0, tiled=True)  132 us
    psum x1, waiting for transfers between devices, local(): summed = lax.psum(left_dot(lower_here, stacked), ('row', 'col'))  83.9 us
    psum x1, waiting for transfers between devices, broadcast(): return lax.psum(kept, axis)  66 us
    dot_general x11, matrix products, matmul(): return jnp.dot(left, right, precision=highest)  36 us
    all_to_all x1, waiting for transfers between devices, local(): lax.all_to_all(slotted, 'col', split_axis=1, concat_axis=1, tiled=True)  21 us
    dot_general x6, matrix products, left_dot(): lax.dot_general(left, right, (((0,), (0,)), ((), ())), precision=highest)  16.5 us
    all_to_all x1, waiting for transfers between devices, local(): lax.all_to_all(split_parts, 'row', split_axis=1, concat_axis=1, tiled=True)  15.6 us
  transfers between devices with their start and end apart: 11, of which 11 were waited for; matrix products, arithmetic and copies ran while one was open for 7% of the time, Pallas kernels for 0%

commit v1 on v0

--- a/solution.py
+++ b/solution.py
@@ -40,7 +40,19 @@
     for current in range(nodes_total):
         listed = jnp.any(ancestors[current][:, None] == block_of_row[None, :], axis=0)
         lower_part = jnp.where(listed[:, None], factor[current], jnp.zeros_like(factor[current]))
-        lower_rows = lax.all_gather(lower_part, "col", axis=0, tiled=True)
+        size_here = lax.psum(1, "col")
+        by_place = tuple(((m, (m + 1) % size_here) for m in range(size_here)))
+        part_now, a_now = ([lower_part], [lower_part])
+        entries = tuple(((m, (m - 1) % size_here) for m in range(size_here)))
+        for _ in range(size_here // 2):
+            part_now.append(lax.ppermute(part_now[-1], "col", by_place))
+        for _ in range((size_here - 1) // 2):
+            a_now.append(lax.ppermute(a_now[-1], "col", entries))
+        lower_rows = jnp.roll(
+            jnp.concatenate([*part_now[::-1], *a_now[1:]], axis=0),
+            (lax.axis_index("col") - size_here // 2) * lower_part.shape[0],
+            axis=0,
+        )
         own_block = lax.dynamic_slice_in_dim(lower_rows, block_start, cols_here, 0)
         lower_cols = broadcast(own_block, "row", source_row).astype(jnp.float32)
         lower_here = lower_part.astype(jnp.float32)

time: 699 us -> 675 us (0.966)
  waiting for transfers between devices: 539 us -> 417 us
  starting transfers between devices: 21.2 us -> 109 us
    all_gather x3 -> x0, waiting for transfers between devices: 132 us -> none  [local(): lower_rows = lax.all_gather(lower_part, 'col', axis=0, tiled=True)]
    ppermute x0 -> x45, starting transfers between devices: none -> 88.1 us  [the longest x21 83.7 us: local(): a_now.append(lax.ppermute(a_now[-1], 'col', entries))]
    psum x1, waiting for transfers between devices: 66 us -> 76.5 us  [broadcast(): return lax.psum(kept, axis)]
    unnamed x50 -> x105, local copies, waits for them, and re-layouts: 14.4 us -> 20.4 us
  transfers between devices with their start and end apart: 11 -> 53, of which waited for: 11 -> 14; matrix products, arithmetic and copies ran while one was open for 7% -> 9% of each run, Pallas kernels for 0% -> 0%
where the time goes in v1:
time: 675 us; the launch traced here: 665 us
  waiting for transfers between devices  417 us (62%)
  starting transfers between devices  109 us (16%)
  matrix products  55.5 us (8%)
  local copies, waits for them, and re-layouts  41.9 us (6%)
  other arithmetic  27 us (4%)
  between operations  15.1 us (2%)
    reduce_scatter x3, waiting for transfers between devices, local(): lax.psum_scatter(matmul(ancestor_inverse, lower_cols), 'col', scatter_dim...  208 us
    psum x1, waiting for transfers between devices, local(): summed = lax.psum(left_dot(lower_here, stacked), ('row', 'col'))  83.8 us
    ppermute x21, starting transfers between devices, local(): a_now.append(lax.ppermute(a_now[-1], 'col', entries))  83.7 us
    psum x1, waiting for transfers between devices, broadcast(): return lax.psum(kept, axis)  76.5 us
    dot_general x11, matrix products, matmul(): return jnp.dot(left, right, precision=highest)  36 us
    all_to_all x1, waiting for transfers between devices, local(): lax.all_to_all(slotted, 'col', split_axis=1, concat_axis=1, tiled=True)  21 us
    unnamed x105, local copies, waits for them, and re-layouts  20.4 us
    dot_general x6, matrix products, left_dot(): lax.dot_general(left, right, (((0,), (0,)), ((), ())), precision=highest)  17.5 us
  transfers between devices with their start and end apart: 53, of which 14 were waited for; matrix products, arithmetic and copies ran while one was open for 9% of the time, Pallas kernels for 0%

profile of v1, /device:TPU:1, one launch (start us, length us, event | category | flops | bytes accessed | tf_op | source)
XLA Modules:
  0.0 665.4 jit_solution(3259473136085064941)
XLA Ops:
  11.4 4.8 collective-permute-start.23
  16.2 4.8 collective-permute-start.8
  21.0 4.8 collective-permute-start.38
  25.8 4.8 collective-permute-start.24
  30.6 4.8 collective-permute-start.9
  35.4 4.8 collective-permute-start.39
  40.2 4.8 collective-permute-start.25
  45.0 4.8 collective-permute-start.10
  49.8 4.8 collective-permute-start.40
  54.6 4.8 collective-permute-start.26
  59.4 4.8 collective-permute-start.11
  64.2 4.8 collective-permute-start.41
  69.0 4.8 collective-permute-start.27
  73.7 4.8 collective-permute-start.12
  78.6 5.0 collective-permute-start.42
  86.4 4.8 collective-permute-start.13
  95.1 4.8 collective-permute-start.29
  109.1 2.4 fusion.41
  111.6 2.4 fusion.43
  115.2 2.4 fusion.39
  118.0 76.5 %all-reduce.7.cloned.1.call-done = (bf16[768,512]{1,0:T(8,128)(2,1)}, bf16[768,512]{1,0:T(8,128)(2,1)}, bf16[768,512]{1,0:T(8,128)(2,1)}) async-done(((bf16[768,512]{1,0:T(8,128)(2,1)}, bf16[768,512]{1,0:T(8,128)(2,1)}, bf16[768,512]{1,0:T(8,128)(2,1)}), (bf16[768,512]{1,0:T(8,128)(2,1)}, bf16[768,512]{1,0:T(8,128)(2,1)}, bf16[768,512]{1,0:T(8,128)(2,1)})) %all-reduce.7.cloned.1.call-update) | async-done | bytes 2359312 | tf_op jit(solution)/shard_map/psum | solution.py:11
  194.5 6.7 %convolution_bitcast_fusion.2 = f32[1536,512]{0,1:T(8,128)S(1)} fusion(bf16[768,512]{1,0:T(8,128)(2,1)} %get-tuple-element.17, f32[1536,768]{1,0:T(8,128)} %param.7), kind=kOutput, calls=%fused_computation.3 | convolution fusion | flops 7247757312 | bytes 8650752 | tf_op jit(solution)/shard_map/dot_general | solution.py:15
  201.2 2.4 copy.104
  203.6 6.7 %convolution_bitcast_fusion.1 = f32[1536,512]{0,1:T(8,128)S(1)} fusion(bf16[768,512]{1,0:T(8,128)(2,1)} %get-tuple-element.18, f32[1536,768]{1,0:T(8,128)} %param.7), kind=kOutput, calls=%fused_computation.2 | convolution fusion | flops 7247757312 | bytes 8650752 | tf_op jit(solution)/shard_map/dot_general | solution.py:15
  210.3 2.4 copy.106
  212.8 6.7 %convolution_bitcast_fusion = f32[1536,512]{0,1:T(8,128)S(1)} fusion(bf16[768,512]{1,0:T(8,128)(2,1)} %get-tuple-element.16, f32[1536,768]{1,0:T(8,128)} %param.7), kind=kOutput, calls=%fused_computation.1 | convolution fusion | flops 7247757312 | bytes 8650752 | tf_op jit(solution)/shard_map/dot_general | solution.py:15
  219.5 2.4 copy.108
  222.1 57.4 %reduce-scatter.10.cloned.1.call-done = f32[96,512]{1,0:T(8,128)} async-done(((f32[1536,512]{1,0:T(8,128)}), f32[96,512]{1,0:T(8,128)}) %reduce-scatter.10.cloned.1.call-update) | async-done | bytes 196624 | tf_op jit(solution)/shard_map/reduce_scatter | solution.py:59
  281.2 76.8 %reduce-scatter.12.cloned.1.call-done = f32[96,512]{1,0:T(8,128)} async-done(((f32[1536,512]{1,0:T(8,128)}), f32[96,512]{1,0:T(8,128)}) %reduce-scatter.12.cloned.1.call-update) | async-done | bytes 196624 | tf_op jit(solution)/shard_map/reduce_scatter | solution.py:59
  359.8 3.3 fusion.51
  363.1 73.7 %reduce-scatter.14.cloned.1.call-done = f32[96,512]{1,0:T(8,128)} async-done(((f32[1536,512]{1,0:T(8,128)}), f32[96,512]{1,0:T(8,128)}) %reduce-scatter.14.cloned.1.call-update) | async-done | bytes 196624 | tf_op jit(solution)/shard_map/reduce_scatter | solution.py:59
  439.4 3.1 fusion.44
  450.3 6.6 all-to-all-start
  456.9 15.7 %all-to-all-done = f32[3,8,12,512]{3,2,0,1:T(8,128)} async-done(((f32[3,8,12,512]{3,2,0,1:T(8,128)}), f32[3,8,12,512]{3,2,0,1:T(8,128)}, u32[]{:S(2)}, u32[]{:S(2)}) %all-to-all-start) | async-done | bytes 589856 | tf_op jit(solution)/shard_map/all_to_all | solution.py:92
  476.6 4.7 all-to-all-start.1
  481.3 21.0 %all-to-all-done.1 = f32[3,16,12,512]{3,2,0,1:T(8,128)} async-done(((f32[3,16,12,512]{3,2,0,1:T(8,128)}), f32[3,16,12,512]{3,2,0,1:T(8,128)}, u32[]{:S(2)}, u32[]{:S(2)}) %all-to-all-start.1) | async-done | bytes 1179680 | tf_op jit(solution)/shard_map/all_to_all | solution.py:98
  504.4 9.1 %all-to-all-start.2 = ((f32[3,8,12,512]{3,2,0,1:T(8,128)}), f32[3,8,12,512]{3,2,0,1:T(8,128)}, u32[]{:S(2)}, u32[]{:S(2)}) async-start(f32[3,8,12,512]{3,2,0,1:T(8,128)} %constant_dynamic-slice_fusion), calls=%async_computation.2 | async-start | bytes 1572864 | tf_op jit(solution)/shard_map/all_to_all | solution.py:100
  513.5 2.3 slice.71
  515.9 2.5 copy.110
  520.2 5.7 all-to-all-done.2
  530.1 83.8 %all-reduce.5.cloned.1.call-done = (f32[512,1536]{1,0:T(8,128)}, f32[512,512]{1,0:T(8,128)}, f32[512,1024]{0,1:T(8,128)}) async-done(((f32[512,1536]{1,0:T(8,128)}, f32[512,512]{1,0:T(8,128)}, f32[512,1024]{0,1:T(8,128)}), (f32[512,1536]{1,0:T(8,128)}, f32[512,512]{1,0:T(8,128)}, f32[512,1024]{0,1:T(8,128)})) %all-reduce.5.cloned.1.call-update) | async-done | bytes 6291472 | tf_op jit(solution)/shard_map/psum | solution.py:68
  614.0 3.8 bitcast_subtract_fusion.7
  628.1 3.1 fusion.2
  635.8 2.6 copy.85
  638.4 3.8 maximum_bitcast_fusion.1
  642.2 3.5 copy.95
  645.8 4.3 fusion.1
  653.5 4.9 pad_maximum_fusion
  (217 shorter events, 66.1 us)
Async XLA Ops:
  7.2 187.3 %all-reduce.7.cloned.1.call-start = ((), (), s32[]{:S(2)}) async-start(), calls=%async_computation.10 | async-start | bytes 4718592 | tf_op jit(solution)/shard_map/psum | solution.py:11
  9.3 11.7 %collective-permute-start.15 = (bf16[96,512]{1,0:T(8,128)(2,1)S(1)}, bf16[96,512]{1,0:T(8,128)(2,1)S(1)}, u32[]{:S(2)}, u32[]{:S(2)}) collective-permute-start(bf16[96,512]{1,0:T(8,128)(2,1)S(1)} %get-tuple-element.23), channel_id=1, source_target_pairs={{0,1},{1,2},{2,3},{3,4},{4,5},{5,6},{6,7},{7,8},{8,9},{9,10},{10,1... | collective-permute-start | bytes 294920 | tf_op jit(solution)/shard_map/ppermute | solution.py:48
  11.4 14.4 %collective-permute-start.23 = (bf16[96,512]{1,0:T(8,128)(2,1)S(1)}, bf16[96,512]{1,0:T(8,128)(2,1)S(1)}, u32[]{:S(2)}, u32[]{:S(2)}) collective-permute-start(bf16[96,512]{1,0:T(8,128)(2,1)S(1)} %get-tuple-element.23), channel_id=1, source_target_pairs={{0,15},{1,0},{2,1},{3,2},{4,3},{5,4},{6,5},{7,6},{8,7},{9,8},{10,9... | collective-permute-start | bytes 294920 | tf_op jit(solution)/shard_map/ppermute | solution.py:50
  16.2 9.6 %collective-permute-start = (bf16[96,512]{1,0:T(8,128)(2,1)S(1)}, bf16[96,512]{1,0:T(8,128)(2,1)S(1)}, u32[]{:S(2)}, u32[]{:S(2)}) collective-permute-start(bf16[96,512]{1,0:T(8,128)(2,1)S(1)} %get-tuple-element.24), channel_id=1, source_target_pairs={{0,1},{1,2},{2,3},{3,4},{4,5},{5,6},{6,7},{7,8},{8,9},{9,10},{10,1... | collective-permute-start | bytes 294920 | tf_op jit(solution)/shard_map/ppermute | solution.py:48
  16.2 14.4 %collective-permute-start.8 = (bf16[96,512]{1,0:T(8,128)(2,1)S(1)}, bf16[96,512]{1,0:T(8,128)(2,1)S(1)}, u32[]{:S(2)}, u32[]{:S(2)}) collective-permute-start(bf16[96,512]{1,0:T(8,128)(2,1)S(1)} %get-tuple-element.24), channel_id=1, source_target_pairs={{0,15},{1,0},{2,1},{3,2},{4,3},{5,4},{6,5},{7,6},{8,7},{9,8},{10,9... | collective-permute-start | bytes 294920 | tf_op jit(solution)/shard_map/ppermute | solution.py:50
  21.0 9.6 %collective-permute-start.30 = (bf16[96,512]{1,0:T(8,128)(2,1)S(1)}, bf16[96,512]{1,0:T(8,128)(2,1)S(1)}, u32[]{:S(2)}, u32[]{:S(2)}) collective-permute-start(bf16[96,512]{1,0:T(8,128)(2,1)S(1)} %get-tuple-element.25), channel_id=1, source_target_pairs={{0,1},{1,2},{2,3},{3,4},{4,5},{5,6},{6,7},{7,8},{8,9},{9,10},{10,1... | collective-permute-start | bytes 294920 | tf_op jit(solution)/shard_map/ppermute | solution.py:48
  21.0 14.4 %collective-permute-start.38 = (bf16[96,512]{1,0:T(8,128)(2,1)S(1)}, bf16[96,512]{1,0:T(8,128)(2,1)S(1)}, u32[]{:S(2)}, u32[]{:S(2)}) collective-permute-start(bf16[96,512]{1,0:T(8,128)(2,1)S(1)} %get-tuple-element.25), channel_id=1, source_target_pairs={{0,15},{1,0},{2,1},{3,2},{4,3},{5,4},{6,5},{7,6},{8,7},{9,8},{10,9... | collective-permute-start | bytes 294920 | tf_op jit(solution)/shard_map/ppermute | solution.py:50
  25.8 9.6 %collective-permute-start.16 = (bf16[96,512]{1,0:T(8,128)(2,1)S(1)}, bf16[96,512]{1,0:T(8,128)(2,1)S(1)}, u32[]{:S(2)}, u32[]{:S(2)}) collective-permute-start(bf16[96,512]{1,0:T(8,128)(2,1)S(1)} %collective-permute-done.15), channel_id=1, source_target_pairs={{0,1},{1,2},{2,3},{3,4},{4,5},{5,6},{6,7},{7,8},{8,9},{9,10},{10,1... | collective-permute-start | bytes 294920 | tf_op jit(solution)/shard_map/ppermute | solution.py:48
  25.8 14.4 %collective-permute-start.24 = (bf16[96,512]{1,0:T(8,128)(2,1)S(1)}, bf16[96,512]{1,0:T(8,128)(2,1)S(1)}, u32[]{:S(2)}, u32[]{:S(2)}) collective-permute-start(bf16[96,512]{1,0:T(8,128)(2,1)S(1)} %collective-permute-done.23), channel_id=1, source_target_pairs={{0,15},{1,0},{2,1},{3,2},{4,3},{5,4},{6,5},{7,6},{8,7},{9,8},{10,9... | collective-permute-start | bytes 294920 | tf_op jit(solution)/shard_map/ppermute | solution.py:50
  30.6 9.6 %collective-permute-start.1 = (bf16[96,512]{1,0:T(8,128)(2,1)S(1)}, bf16[96,512]{1,0:T(8,128)(2,1)S(1)}, u32[]{:S(2)}, u32[]{:S(2)}) collective-permute-start(bf16[96,512]{1,0:T(8,128)(2,1)S(1)} %collective-permute-done), channel_id=1, source_target_pairs={{0,1},{1,2},{2,3},{3,4},{4,5},{5,6},{6,7},{7,8},{8,9},{9,10},{10,1... | collective-permute-start | bytes 294920 | tf_op jit(solution)/shard_map/ppermute | solution.py:48
  30.6 14.4 %collective-permute-start.9 = (bf16[96,512]{1,0:T(8,128)(2,1)S(1)}, bf16[96,512]{1,0:T(8,128)(2,1)S(1)}, u32[]{:S(2)}, u32[]{:S(2)}) collective-permute-start(bf16[96,512]{1,0:T(8,128)(2,1)S(1)} %collective-permute-done.8), channel_id=1, source_target_pairs={{0,15},{1,0},{2,1},{3,2},{4,3},{5,4},{6,5},{7,6},{8,7},{9,8},{10,9... | collective-permute-start | bytes 294920 | tf_op jit(solution)/shard_map/ppermute | solution.py:50
  35.4 9.6 %collective-permute-start.31 = (bf16[96,512]{1,0:T(8,128)(2,1)S(1)}, bf16[96,512]{1,0:T(8,128)(2,1)S(1)}, u32[]{:S(2)}, u32[]{:S(2)}) collective-permute-start(bf16[96,512]{1,0:T(8,128)(2,1)S(1)} %collective-permute-done.30), channel_id=1, source_target_pairs={{0,1},{1,2},{2,3},{3,4},{4,5},{5,6},{6,7},{7,8},{8,9},{9,10},{10,1... | collective-permute-start | bytes 294920 | tf_op jit(solution)/shard_map/ppermute | solution.py:48
  35.4 14.4 %collective-permute-start.39 = (bf16[96,512]{1,0:T(8,128)(2,1)S(1)}, bf16[96,512]{1,0:T(8,128)(2,1)S(1)}, u32[]{:S(2)}, u32[]{:S(2)}) collective-permute-start(bf16[96,512]{1,0:T(8,128)(2,1)S(1)} %collective-permute-done.38), channel_id=1, source_target_pairs={{0,15},{1,0},{2,1},{3,2},{4,3},{5,4},{6,5},{7,6},{8,7},{9,8},{10,9... | collective-permute-start | bytes 294920 | tf_op jit(solution)/shard_map/ppermute | solution.py:50
  40.2 9.6 %collective-permute-start.17 = (bf16[96,512]{1,0:T(8,128)(2,1)S(1)}, bf16[96,512]{1,0:T(8,128)(2,1)S(1)}, u32[]{:S(2)}, u32[]{:S(2)}) collective-permute-start(bf16[96,512]{1,0:T(8,128)(2,1)S(1)} %collective-permute-done.16), channel_id=1, source_target_pairs={{0,1},{1,2},{2,3},{3,4},{4,5},{5,6},{6,7},{7,8},{8,9},{9,10},{10,1... | collective-permute-start | bytes 294920 | tf_op jit(solution)/shard_map/ppermute | solution.py:48
  40.2 14.4 %collective-permute-start.25 = (bf16[96,512]{1,0:T(8,128)(2,1)S(1)}, bf16[96,512]{1,0:T(8,128)(2,1)S(1)}, u32[]{:S(2)}, u32[]{:S(2)}) collective-permute-start(bf16[96,512]{1,0:T(8,128)(2,1)S(1)} %collective-permute-done.24), channel_id=1, source_target_pairs={{0,15},{1,0},{2,1},{3,2},{4,3},{5,4},{6,5},{7,6},{8,7},{9,8},{10,9... | collective-permute-start | bytes 294920 | tf_op jit(solution)/shard_map/ppermute | solution.py:50
  45.0 9.6 %collective-permute-start.2 = (bf16[96,512]{1,0:T(8,128)(2,1)S(1)}, bf16[96,512]{1,0:T(8,128)(2,1)S(1)}, u32[]{:S(2)}, u32[]{:S(2)}) collective-permute-start(bf16[96,512]{1,0:T(8,128)(2,1)S(1)} %collective-permute-done.1), channel_id=1, source_target_pairs={{0,1},{1,2},{2,3},{3,4},{4,5},{5,6},{6,7},{7,8},{8,9},{9,10},{10,1... | collective-permute-start | bytes 294920 | tf_op jit(solution)/shard_map/ppermute | solution.py:48
  45.0 14.4 %collective-permute-start.10 = (bf16[96,512]{1,0:T(8,128)(2,1)S(1)}, bf16[96,512]{1,0:T(8,128)(2,1)S(1)}, u32[]{:S(2)}, u32[]{:S(2)}) collective-permute-start(bf16[96,512]{1,0:T(8,128)(2,1)S(1)} %collective-permute-done.9), channel_id=1, source_target_pairs={{0,15},{1,0},{2,1},{3,2},{4,3},{5,4},{6,5},{7,6},{8,7},{9,8},{10,9... | collective-permute-start | bytes 294920 | tf_op jit(solution)/shard_map/ppermute | solution.py:50
  49.8 9.6 %collective-permute-start.32 = (bf16[96,512]{1,0:T(8,128)(2,1)S(1)}, bf16[96,512]{1,0:T(8,128)(2,1)S(1)}, u32[]{:S(2)}, u32[]{:S(2)}) collective-permute-start(bf16[96,512]{1,0:T(8,128)(2,1)S(1)} %collective-permute-done.31), channel_id=1, source_target_pairs={{0,1},{1,2},{2,3},{3,4},{4,5},{5,6},{6,7},{7,8},{8,9},{9,10},{10,1... | collective-permute-start | bytes 294920 | tf_op jit(solution)/shard_map/ppermute | solution.py:48
  49.8 14.4 %collective-permute-start.40 = (bf16[96,512]{1,0:T(8,128)(2,1)S(1)}, bf16[96,512]{1,0:T(8,128)(2,1)S(1)}, u32[]{:S(2)}, u32[]{:S(2)}) collective-permute-start(bf16[96,512]{1,0:T(8,128)(2,1)S(1)} %collective-permute-done.39), channel_id=1, source_target_pairs={{0,15},{1,0},{2,1},{3,2},{4,3},{5,4},{6,5},{7,6},{8,7},{9,8},{10,9... | collective-permute-start | bytes 294920 | tf_op jit(solution)/shard_map/ppermute | solution.py:50
  54.5 9.6 %collective-permute-start.18 = (bf16[96,512]{1,0:T(8,128)(2,1)S(1)}, bf16[96,512]{1,0:T(8,128)(2,1)S(1)}, u32[]{:S(2)}, u32[]{:S(2)}) collective-permute-start(bf16[96,512]{1,0:T(8,128)(2,1)S(1)} %collective-permute-done.17), channel_id=1, source_target_pairs={{0,1},{1,2},{2,3},{3,4},{4,5},{5,6},{6,7},{7,8},{8,9},{9,10},{10,1... | collective-permute-start | bytes 294920 | tf_op jit(solution)/shard_map/ppermute | solution.py:48
  54.6 14.4 %collective-permute-start.26 = (bf16[96,512]{1,0:T(8,128)(2,1)S(1)}, bf16[96,512]{1,0:T(8,128)(2,1)S(1)}, u32[]{:S(2)}, u32[]{:S(2)}) collective-permute-start(bf16[96,512]{1,0:T(8,128)(2,1)S(1)} %collective-permute-done.25), channel_id=1, source_target_pairs={{0,15},{1,0},{2,1},{3,2},{4,3},{5,4},{6,5},{7,6},{8,7},{9,8},{10,9... | collective-permute-start | bytes 294920 | tf_op jit(solution)/shard_map/ppermute | solution.py:50
  59.4 9.6 %collective-permute-start.3 = (bf16[96,512]{1,0:T(8,128)(2,1)S(1)}, bf16[96,512]{1,0:T(8,128)(2,1)S(1)}, u32[]{:S(2)}, u32[]{:S(2)}) collective-permute-start(bf16[96,512]{1,0:T(8,128)(2,1)S(1)} %collective-permute-done.2), channel_id=1, source_target_pairs={{0,1},{1,2},{2,3},{3,4},{4,5},{5,6},{6,7},{7,8},{8,9},{9,10},{10,1... | collective-permute-start | bytes 294920 | tf_op jit(solution)/shard_map/ppermute | solution.py:48
  59.4 14.4 %collective-permute-start.11 = (bf16[96,512]{1,0:T(8,128)(2,1)S(1)}, bf16[96,512]{1,0:T(8,128)(2,1)S(1)}, u32[]{:S(2)}, u32[]{:S(2)}) collective-permute-start(bf16[96,512]{1,0:T(8,128)(2,1)S(1)} %collective-permute-done.10), channel_id=1, source_target_pairs={{0,15},{1,0},{2,1},{3,2},{4,3},{5,4},{6,5},{7,6},{8,7},{9,8},{10,9... | collective-permute-start | bytes 294920 | tf_op jit(solution)/shard_map/ppermute | solution.py:50
  64.1 9.6 %collective-permute-start.33 = (bf16[96,512]{1,0:T(8,128)(2,1)S(1)}, bf16[96,512]{1,0:T(8,128)(2,1)S(1)}, u32[]{:S(2)}, u32[]{:S(2)}) collective-permute-start(bf16[96,512]{1,0:T(8,128)(2,1)S(1)} %collective-permute-done.32), channel_id=1, source_target_pairs={{0,1},{1,2},{2,3},{3,4},{4,5},{5,6},{6,7},{7,8},{8,9},{9,10},{10,1... | collective-permute-start | bytes 294920 | tf_op jit(solution)/shard_map/ppermute | solution.py:48
  64.2 14.4 %collective-permute-start.41 = (bf16[96,512]{1,0:T(8,128)(2,1)S(1)}, bf16[96,512]{1,0:T(8,128)(2,1)S(1)}, u32[]{:S(2)}, u32[]{:S(2)}) collective-permute-start(bf16[96,512]{1,0:T(8,128)(2,1)S(1)} %collective-permute-done.40), channel_id=1, source_target_pairs={{0,15},{1,0},{2,1},{3,2},{4,3},{5,4},{6,5},{7,6},{8,7},{9,8},{10,9... | collective-permute-start | bytes 294920 | tf_op jit(solution)/shard_map/ppermute | solution.py:50
  68.9 9.6 %collective-permute-start.19 = (bf16[96,512]{1,0:T(8,128)(2,1)S(1)}, bf16[96,512]{1,0:T(8,128)(2,1)S(1)}, u32[]{:S(2)}, u32[]{:S(2)}) collective-permute-start(bf16[96,512]{1,0:T(8,128)(2,1)S(1)} %collective-permute-done.18), channel_id=1, source_target_pairs={{0,1},{1,2},{2,3},{3,4},{4,5},{5,6},{6,7},{7,8},{8,9},{9,10},{10,1... | collective-permute-start | bytes 294920 | tf_op jit(solution)/shard_map/ppermute | solution.py:48
  69.0 9.7 %collective-permute-start.27 = (bf16[96,512]{1,0:T(8,128)(2,1)S(1)}, bf16[96,512]{1,0:T(8,128)(2,1)S(1)}, u32[]{:S(2)}, u32[]{:S(2)}) collective-permute-start(bf16[96,512]{1,0:T(8,128)(2,1)S(1)} %collective-permute-done.26), channel_id=1, source_target_pairs={{0,15},{1,0},{2,1},{3,2},{4,3},{5,4},{6,5},{7,6},{8,7},{9,8},{10,9... | collective-permute-start | bytes 294920 | tf_op jit(solution)/shard_map/ppermute | solution.py:50
  73.7 9.9 %collective-permute-start.4 = (bf16[96,512]{1,0:T(8,128)(2,1)S(1)}, bf16[96,512]{1,0:T(8,128)(2,1)S(1)}, u32[]{:S(2)}, u32[]{:S(2)}) collective-permute-start(bf16[96,512]{1,0:T(8,128)(2,1)S(1)} %collective-permute-done.3), channel_id=1, source_target_pairs={{0,1},{1,2},{2,3},{3,4},{4,5},{5,6},{6,7},{7,8},{8,9},{9,10},{10,1... | collective-permute-start | bytes 294920 | tf_op jit(solution)/shard_map/ppermute | solution.py:48
  73.7 11.2 %collective-permute-start.12 = (bf16[96,512]{1,0:T(8,128)(2,1)S(1)}, bf16[96,512]{1,0:T(8,128)(2,1)S(1)}, u32[]{:S(2)}, u32[]{:S(2)}) collective-permute-start(bf16[96,512]{1,0:T(8,128)(2,1)S(1)} %collective-permute-done.11), channel_id=1, source_target_pairs={{0,15},{1,0},{2,1},{3,2},{4,3},{5,4},{6,5},{7,6},{8,7},{9,8},{10,9... | collective-permute-start | bytes 294920 | tf_op jit(solution)/shard_map/ppermute | solution.py:50
  78.6 7.8 %collective-permute-start.20 = (bf16[96,512]{1,0:T(8,128)(2,1)S(1)}, bf16[96,512]{1,0:T(8,128)(2,1)S(1)}, u32[]{:S(2)}, u32[]{:S(2)}) collective-permute-start(bf16[96,512]{1,0:T(8,128)(2,1)S(1)} %collective-permute-done.19), channel_id=1, source_target_pairs={{0,1},{1,2},{2,3},{3,4},{4,5},{5,6},{6,7},{7,8},{8,9},{9,10},{10,1... | collective-permute-start | bytes 294920 | tf_op jit(solution)/shard_map/ppermute | solution.py:48
  78.6 7.7 %collective-permute-start.42 = (bf16[96,512]{1,0:T(8,128)(2,1)S(1)}, bf16[96,512]{1,0:T(8,128)(2,1)S(1)}, u32[]{:S(2)}, u32[]{:S(2)}) collective-permute-start(bf16[96,512]{1,0:T(8,128)(2,1)S(1)} %collective-permute-done.41), channel_id=1, source_target_pairs={{0,15},{1,0},{2,1},{3,2},{4,3},{5,4},{6,5},{7,6},{8,7},{9,8},{10,9... | collective-permute-start | bytes 294920 | tf_op jit(solution)/shard_map/ppermute | solution.py:50
  83.6 7.5 %collective-permute-start.28 = (bf16[96,512]{1,0:T(8,128)(2,1)S(1)}, bf16[96,512]{1,0:T(8,128)(2,1)S(1)}, u32[]{:S(2)}, u32[]{:S(2)}) collective-permute-start(bf16[96,512]{1,0:T(8,128)(2,1)S(1)} %collective-permute-done.27), channel_id=1, source_target_pairs={{0,15},{1,0},{2,1},{3,2},{4,3},{5,4},{6,5},{7,6},{8,7},{9,8},{10,9... | collective-permute-start | bytes 294920 | tf_op jit(solution)/shard_map/ppermute | solution.py:50
  86.4 8.7 %collective-permute-start.21 = (bf16[96,512]{1,0:T(8,128)(2,1)S(1)}, bf16[96,512]{1,0:T(8,128)(2,1)}, u32[]{:S(2)}, u32[]{:S(2)}) collective-permute-start(bf16[96,512]{1,0:T(8,128)(2,1)S(1)} %collective-permute-done.20), channel_id=1, source_target_pairs={{0,1},{1,2},{2,3},{3,4},{4,5},{5,6},{6,7},{7,8},{8,9},{9,10},{10,1... | collective-permute-start | bytes 294920 | tf_op jit(solution)/shard_map/ppermute | solution.py:48
  86.4 8.7 %collective-permute-start.13 = (bf16[96,512]{1,0:T(8,128)(2,1)S(1)}, bf16[96,512]{1,0:T(8,128)(2,1)S(1)}, u32[]{:S(2)}, u32[]{:S(2)}) collective-permute-start(bf16[96,512]{1,0:T(8,128)(2,1)S(1)} %collective-permute-done.12), channel_id=1, source_target_pairs={{0,15},{1,0},{2,1},{3,2},{4,3},{5,4},{6,5},{7,6},{8,7},{9,8},{10,9... | collective-permute-start | bytes 294920 | tf_op jit(solution)/shard_map/ppermute | solution.py:50
  91.2 8.7 %collective-permute-start.43 = (bf16[96,512]{1,0:T(8,128)(2,1)S(1)}, bf16[96,512]{1,0:T(8,128)(2,1)S(1)}, u32[]{:S(2)}, u32[]{:S(2)}) collective-permute-start(bf16[96,512]{1,0:T(8,128)(2,1)S(1)} %collective-permute-done.42), channel_id=1, source_target_pairs={{0,15},{1,0},{2,1},{3,2},{4,3},{5,4},{6,5},{7,6},{8,7},{9,8},{10,9... | collective-permute-start | bytes 294920 | tf_op jit(solution)/shard_map/ppermute | solution.py:50
  91.9 8.0 %collective-permute-start.6 = (bf16[96,512]{1,0:T(8,128)(2,1)}, bf16[96,512]{1,0:T(8,128)(2,1)}, u32[]{:S(2)}, u32[]{:S(2)}) collective-permute-start(bf16[96,512]{1,0:T(8,128)(2,1)} %collective-permute-done.5), channel_id=1, source_target_pairs={{0,1},{1,2},{2,3},{3,4},{4,5},{5,6},{6,7},{7,8},{8,9},{9,10},{10,1... | collective-permute-start | bytes 294920 | tf_op jit(solution)/shard_map/ppermute | solution.py:48
  95.1 8.3 %collective-permute-start.22 = (bf16[96,512]{1,0:T(8,128)(2,1)}, bf16[96,512]{1,0:T(8,128)(2,1)}, u32[]{:S(2)}, u32[]{:S(2)}) collective-permute-start(bf16[96,512]{1,0:T(8,128)(2,1)} %collective-permute-done.21), channel_id=1, source_target_pairs={{0,1},{1,2},{2,3},{3,4},{4,5},{5,6},{6,7},{7,8},{8,9},{9,10},{10,1... | collective-permute-start | bytes 294920 | tf_op jit(solution)/shard_map/ppermute | solution.py:48
  95.1 14.0 %collective-permute-start.29 = (bf16[96,512]{1,0:T(8,128)(2,1)S(1)}, bf16[96,512]{1,0:T(8,128)(2,1)S(1)}, u32[]{:S(2)}, u32[]{:S(2)}) collective-permute-start(bf16[96,512]{1,0:T(8,128)(2,1)S(1)} %collective-permute-done.28), channel_id=1, source_target_pairs={{0,15},{1,0},{2,1},{3,2},{4,3},{5,4},{6,5},{7,6},{8,7},{9,8},{10,9... | collective-permute-start | bytes 294920 | tf_op jit(solution)/shard_map/ppermute | solution.py:50
  99.8 11.7 %collective-permute-start.14 = (bf16[96,512]{1,0:T(8,128)(2,1)S(1)}, bf16[96,512]{1,0:T(8,128)(2,1)S(1)}, u32[]{:S(2)}, u32[]{:S(2)}) collective-permute-start(bf16[96,512]{1,0:T(8,128)(2,1)S(1)} %collective-permute-done.13), channel_id=1, source_target_pairs={{0,15},{1,0},{2,1},{3,2},{4,3},{5,4},{6,5},{7,6},{8,7},{9,8},{10,9... | collective-permute-start | bytes 294920 | tf_op jit(solution)/shard_map/ppermute | solution.py:50
  99.9 15.2 %collective-permute-start.44 = (bf16[96,512]{1,0:T(8,128)(2,1)S(1)}, bf16[96,512]{1,0:T(8,128)(2,1)S(1)}, u32[]{:S(2)}, u32[]{:S(2)}) collective-permute-start(bf16[96,512]{1,0:T(8,128)(2,1)S(1)} %collective-permute-done.43), channel_id=1, source_target_pairs={{0,15},{1,0},{2,1},{3,2},{4,3},{5,4},{6,5},{7,6},{8,7},{9,8},{10,9... | collective-permute-start | bytes 294920 | tf_op jit(solution)/shard_map/ppermute | solution.py:50
  103.3 10.7 %collective-permute-start.37 = (bf16[96,512]{1,0:T(8,128)(2,1)}, bf16[96,512]{1,0:T(8,128)(2,1)S(1)}, u32[]{:S(2)}, u32[]{:S(2)}) collective-permute-start(bf16[96,512]{1,0:T(8,128)(2,1)} %collective-permute-done.36), channel_id=1, source_target_pairs={{0,1},{1,2},{2,3},{3,4},{4,5},{5,6},{6,7},{7,8},{8,9},{9,10},{10,1... | collective-permute-start | bytes 294920 | tf_op jit(solution)/shard_map/ppermute | solution.py:48
  117.6 161.9 %reduce-scatter.10.cloned.1.call-start = ((), (), s32[]{:S(2)}) async-start(), calls=%async_computation.6 | async-start | bytes 3342336 | tf_op jit(solution)/shard_map/reduce_scatter | solution.py:59
  203.6 154.4 %reduce-scatter.12.cloned.1.call-start = ((), (), s32[]{:S(2)}) async-start(), calls=%async_computation.7 | async-start | bytes 3342336 | tf_op jit(solution)/shard_map/reduce_scatter | solution.py:59
  212.7 224.1 %reduce-scatter.14.cloned.1.call-start = ((), (), s32[]{:S(2)}) async-start(), calls=%async_computation.8 | async-start | bytes 3342336 | tf_op jit(solution)/shard_map/reduce_scatter | solution.py:59
  221.9 392.1 %all-reduce.5.cloned.1.call-start = ((), (), s32[]{:S(2)}) async-start(), calls=%async_computation.9 | async-start | bytes 12582912 | tf_op jit(solution)/shard_map/psum | solution.py:68
  450.3 22.4 %all-to-all-start = ((f32[3,8,12,512]{3,2,0,1:T(8,128)}), f32[3,8,12,512]{3,2,0,1:T(8,128)}, u32[]{:S(2)}, u32[]{:S(2)}) async-start(f32[3,8,12,512]{3,2,0,1:T(8,128)} %copy.78), calls=%async_computation | async-start | bytes 1572864 | tf_op jit(solution)/shard_map/all_to_all | solution.py:92
  476.6 25.7 %all-to-all-start.1 = ((f32[3,16,12,512]{3,2,0,1:T(8,128)}), f32[3,16,12,512]{3,2,0,1:T(8,128)}, u32[]{:S(2)}, u32[]{:S(2)}) async-start(f32[3,16,12,512]{3,2,0,1:T(8,128)} %copy.80), calls=%async_computation.1 | async-start | bytes 3145728 | tf_op jit(solution)/shard_map/all_to_all | solution.py:98
  504.4 21.5 %all-to-all-start.2 = ((f32[3,8,12,512]{3,2,0,1:T(8,128)}), f32[3,8,12,512]{3,2,0,1:T(8,128)}, u32[]{:S(2)}, u32[]{:S(2)}) async-start(f32[3,8,12,512]{3,2,0,1:T(8,128)} %constant_dynamic-slice_fusion), calls=%async_computation.2 | async-start | bytes 1572864 | tf_op jit(solution)/shard_map/all_to_all | solution.py:100
  (33 other events, 642.1 us)
Sparse Core Ops, SparseCore 0:
  117.7 76.7 all-reduce.6
  203.7 75.7 reduce-scatter.9
  282.8 75.0 reduce-scatter.11
  361.7 75.0 reduce-scatter.13
  444.3 169.6 all-reduce.4
